TPU v7x, 32 devices: a whole 2x2x4 slice. The times are simulated.
32 devices in a mesh: seg: 2 (over y), ch: 16 (over z, x, core).
Axes of the slice: x: 2, y: 2, z: 4, core: 2. Of those that a mesh axis runs over, the one named last changes fastest.
Arguments:
- strain: float32 [2, 1024, 2048], P('seg', 'ch')
- ref_local: int32 [4, 16], replicated, may hold values from 0 to 127, as said below
- owners: int32 [4], replicated, may hold values from 0 to 15, as said below
Outputs:
- toeplitz_blocks: float32 [64, 2048, 64], P('seg', 'ch')
Inputs may be any that keep to these rules, and one draw needn't show every extreme that they name: `ref_local`: each row holds 16 distinct offsets; the first row holds 127. `owners`: the 4 entries are distinct, and one of them is 15.
All inputs are finite; a program needn't handle non-finite values.
Results may differ from a plain program's by a relative error of at most 0.0029.
Values may be sent and summed in bfloat16 or wider, within the bound.
A program may use at most 64 MiB of HBM per device.

v0:
```python
import jax
import jax.numpy as jnp
from jax import lax
from jax.sharding import PartitionSpec as P

L = 64


def spread_2(block, axis, holder):
    block = jnp.where(lax.axis_index(axis) == holder, block, jnp.zeros_like(block))
    return lax.psum(block, axis)


def detrend_cols(series):
    n_total = series.shape[0]
    mid_time = (n_total - 1) / 2.0
    spread = n_total * (n_total * n_total - 1) / 12.0
    centred = (jnp.arange(n_total, dtype=jnp.float32) - mid_time)[:, None]
    level_val = jnp.sum(series, axis=0) / n_total
    slope_val = jnp.sum(centred * series, axis=0) / spread
    return (series - level_val - slope_val * centred).astype(jnp.bfloat16)


def owner_panels(detrended, ref_local, owners):
    pieces = []
    for panel_id in range(ref_local.shape[0]):
        own_cols = jnp.take(detrended, ref_local[panel_id], axis=1)
        pieces.append(spread_2(own_cols, "ch", owners[panel_id]))
    return jnp.concatenate(pieces, axis=1)


def per_device(strain, ref_local, owners):
    my_rows = strain[0]
    s_dev, chans = my_rows.shape
    n_ch = lax.axis_size("ch")
    n_seg = lax.axis_size("seg")
    n_total = s_dev * n_ch
    c_dev = chans // n_ch
    series = lax.all_to_all(my_rows, "ch", split_axis=1, concat_axis=0, tiled=True)
    detrended = detrend_cols(series)
    panels = owner_panels(detrended, ref_local, owners)
    width_ref = panels.shape[1]
    padded = jnp.concatenate([detrended, jnp.zeros((L, c_dev), jnp.bfloat16)], axis=0)
    blk_rows = min(512, n_total)
    n_blocks = n_total // blk_rows
    lag_dev = L // n_seg
    lag_count = lax.axis_size("seg") * lag_dev

    def add_block(blk_idx, running):
        blk_start = blk_idx * blk_rows
        window = lax.dynamic_slice_in_dim(padded, blk_start, blk_rows + lag_count - 1, 0)
        lagged = jnp.concatenate(
            [window[lag_off : lag_off + blk_rows] for lag_off in range(lag_count)], axis=1
        )
        ref_block = lax.dynamic_slice_in_dim(panels, blk_start, blk_rows, 0)
        return running + lax.dot_general(
            lagged, ref_block, (((0,), (0,)), ((), ())), preferred_element_type=jnp.float32
        )

    start_acc = jnp.zeros((lag_count * c_dev, width_ref), jnp.float32)
    running = lax.fori_loop(0, n_blocks, add_block, start_acc)
    summed = lax.psum_scatter(
        running.reshape(lag_count, c_dev, width_ref), "seg", scatter_dimension=0, tiled=True
    )
    lag_ids = (lax.axis_index("seg") * lag_dev + jnp.arange(lag_dev, dtype=jnp.int32)).astype(
        jnp.float32
    )
    return summed / (n_seg * (n_total - lag_ids))[:, None, None]


def solution(mesh):
    in_specs = (P("seg", "ch", None), P(), P())
    out_specs = P("seg", "ch", None)
    return jax.shard_map(
        per_device, mesh=mesh, in_specs=in_specs, out_specs=out_specs, check_vma=False
    )
```

profile of v0, /device:TPU:0, one launch (start us, length us, event | category | flops | bytes accessed | tf_op | source)
XLA Modules:
  0.0 272.1 jit_solution(4993539267196957720)
XLA Ops:
  6.5 1.1 copy.23
  7.7 1.0 copy.16
  8.6 7.4 %all-to-all-start = ((f32[64,16,128]{2,0,1:T(8,128)}), f32[64,16,128]{2,0,1:T(8,128)S(1)}, u32[]{:S(2)}, u32[]{:S(2)}) async-start(f32[64,16,128]{2,0,1:T(8,128)} %copy.16), calls=%async_computation | async-start | bytes 1048576 | tf_op jit(solution)/shard_map/all_to_all | solution.py:39
  16.1 1.5 fusion.3
  20.0 0.8 compare_and_fusion.3
  20.9 9.4 %all-to-all-done = f32[64,16,128]{2,0,1:T(8,128)S(1)} async-done(((f32[64,16,128]{2,0,1:T(8,128)}), f32[64,16,128]{2,0,1:T(8,128)S(1)}, u32[]{:S(2)}, u32[]{:S(2)}) %all-to-all-start) | async-done | bytes 524320 | tf_op jit(solution)/shard_map/all_to_all | solution.py:39
  36.4 88.2 %all-reduce.4.cloned.1.call-done = (bf16[1024,16]{0,1:T(8,128)(2,1)}, bf16[1024,16]{0,1:T(8,128)(2,1)}, bf16[1024,16]{0,1:T(8,128)(2,1)}, bf16[1024,16]{0,1:T(8,128)(2,1)}) async-done(((bf16[1024,16]{0,1:T(8,128)(2,1)}, bf16[1024,16]{0,1:T(8,128)(2,1)}, bf16[1024,16]{0,1:T(8,128)(2,1)}, bf16[1024,16]{0,1:T(8,128)(2,1)}), (bf16[1024,16]{0,1:T(8,128)(2,1)}, bf16[1024,16]{0,1:T(8,128)(2,1)}, ...) | async-done | bytes 131088 | tf_op jit(solution)/shard_map/psum | solution.py:11
  124.6 0.8 pad_maximum_fusion
  125.4 101.3 %while.14 = (s32[]{:T(128)}, f32[8192,64]{0,1:T(8,128)S(1)}, bf16[1088,128]{1,0:T(8,128)(2,1)S(1)}, bf16[1024,64]{0,1:T(8,128)(2,1)S(1)}, s32[]{:T(128)}, /*inde...) while((s32[]{:T(128)}, f32[8192,64]{0,1:T(8,128)S(1)}, ...), condition=%wide.region_7.9_spmd.clone, body=%wide.region_6.8_spmd.clone.sunk | while | flops 537919552 | bytes 29427356 | solution.py:61
  135.3 0.8 constant_dynamic-update-slice_fusion.142
  143.1 0.7 constant_dynamic-update-slice_fusion.153
  146.7 0.8 constant_dynamic-update-slice_fusion.158
  150.3 0.8 constant_dynamic-update-slice_fusion.163
  163.1 0.8 constant_dynamic-update-slice_fusion.181
  170.9 5.2 %convolution_add_fusion.2 = f32[8192,64]{0,1:T(8,128)S(1)} fusion(bf16[512,8192]{1,0:T(8,128)(2,1)} %constant_dynamic-update-slice_fusion.191, f32[8192,64]{0,1:T(8,128)S(1)} %get-tuple-element.251, pred[]{:T(512)S(6)} %compare.4, bf16[1024,64]{0,1:T(8,128)(2,1)S(1)} %get-tuple-element.325, s32[]{:T(128)S(6)} %select_n.98), kind=kOutput, calls=%fused_computation.4.clone.1 | convolution fusion | flops 537919488 | bytes 12648453 | tf_op jit(solution)/shard_map/while/body/eval_jaxpr/dot_general | solution.py:56
  185.9 0.8 constant_dynamic-update-slice_fusion.142
  197.3 0.8 constant_dynamic-update-slice_fusion.158
  200.9 0.8 constant_dynamic-update-slice_fusion.163
  213.7 0.8 constant_dynamic-update-slice_fusion.181
  221.5 5.2 %convolution_add_fusion.2 = f32[8192,64]{0,1:T(8,128)S(1)} fusion(bf16[512,8192]{1,0:T(8,128)(2,1)} %constant_dynamic-update-slice_fusion.191, f32[8192,64]{0,1:T(8,128)S(1)} %get-tuple-element.251, pred[]{:T(512)S(6)} %compare.4, bf16[1024,64]{0,1:T(8,128)(2,1)S(1)} %get-tuple-element.325, s32[]{:T(128)S(6)} %select_n.98), kind=kOutput, calls=%fused_computation.4.clone.1 | convolution fusion | flops 537919488 | bytes 12648453 | tf_op jit(solution)/shard_map/while/body/eval_jaxpr/dot_general | solution.py:56
  226.7 1.7 copy.24
  228.5 33.8 %reduce-scatter.2.cloned.1.call-done = f32[32,128,64]{1,0,2:T(8,128)} async-done(((f32[64,128,64]{1,0,2:T(8,128)}), f32[32,128,64]{1,0,2:T(8,128)}) %reduce-scatter.2.cloned.1.call-update) | async-done | bytes 1048592 | tf_op jit(solution)/shard_map/reduce_scatter | solution.py:62
  262.3 1.4 broadcast_divide_fusion
  263.7 1.6 copy.20
  (144 shorter events, 90.2 us)
Async XLA Ops:
  8.6 21.7 %all-to-all-start = ((f32[64,16,128]{2,0,1:T(8,128)}), f32[64,16,128]{2,0,1:T(8,128)S(1)}, u32[]{:S(2)}, u32[]{:S(2)}) async-start(f32[64,16,128]{2,0,1:T(8,128)} %copy.16), calls=%async_computation | async-start | bytes 1048576 | tf_op jit(solution)/shard_map/all_to_all | solution.py:39
  16.0 108.6 %all-reduce.4.cloned.1.call-start = ((), (), s32[]{:S(2)}) async-start(), calls=%async_computation.3 | async-start | bytes 262144 | tf_op jit(solution)/shard_map/psum | solution.py:11
  36.2 226.1 %reduce-scatter.2.cloned.1.call-start = ((), (), s32[]{:S(2)}) async-start(), calls=%async_computation.2 | async-start | bytes 3145728 | tf_op jit(solution)/shard_map/reduce_scatter | solution.py:62
Sparse Core Ops, SparseCore 0:
  36.3 88.2 all-reduce.3
  228.6 33.6 reduce-scatter.1
where the time goes:
time: 273 us; the launch traced here: 272 us
  waiting for transfers between devices  131 us (48%)
  local copies, waits for them, and re-layouts  100 us (37%)
  between operations  16 us (6%)
  matrix products  10.4 us (4%)
  starting transfers between devices  7.47 us (3%)
  other arithmetic  6.38 us (2%)
    while x126, local copies, waits for them, and re-layouts  89.4 us
    psum x1, waiting for transfers between devices, spread_2(): return lax.psum(block, axis)  88.2 us
    reduce_scatter x1, waiting for transfers between devices, per_device(): lax.psum_scatter(running.reshape(lag_count, c_dev, width_ref), 'seg', sca...  33.8 us
    dot_general x2, matrix products, add_block(): lax.dot_general(lagged, ref_block, (((0,), (0,)), ((), ())), preferred_el...  10.4 us
    all_to_all x1, waiting for transfers between devices, per_device(): lax.all_to_all(my_rows, 'ch', split_axis=1, concat_axis=0, tiled=True)  9.4 us
    all_to_all x1, starting transfers between devices, per_device(): lax.all_to_all(my_rows, 'ch', split_axis=1, concat_axis=0, tiled=True)  7.39 us
  transfers between devices with their start and end apart: 3, of which 3 were waited for; matrix products, arithmetic and copies ran while one was open for 1% of the time, Pallas kernels for 0%

commit v1 on v0

--- a/solution.py
+++ b/solution.py
@@ -8,7 +8,7 @@
 
 def spread_2(block, axis, holder):
     block = jnp.where(lax.axis_index(axis) == holder, block, jnp.zeros_like(block))
-    return lax.psum(block, axis)
+    return jax.lax.all_gather(block, axis_name=axis).sum(axis=0)
 
 
 def detrend_cols(series):

time: 273 us -> 259 us (0.949)
  waiting for transfers between devices: 131 us -> 39.8 us
  blocking collectives: 0 us -> 79.4 us
    psum x1 -> x0, waiting for transfers between devices: 88.2 us -> none  [spread_2(): return lax.psum(block, axis)]
    all_gather x0 -> x4, blocking collectives: none -> 79.4 us  [spread_2(): return jax.lax.all_gather(block, axis_name=axis).sum(axis=0)]
    reduce_scatter x1, waiting for transfers between devices: 33.8 us -> 30.4 us  [per_device(): lax.psum_scatter(running.reshape(lag_count, c_dev, width_ref), 'seg', sca...]
  transfers between devices with their start and end apart: 3 -> 2, of which waited for: 3 -> 2; matrix products, arithmetic and copies ran while one was open for 1% -> 1% of each run, Pallas kernels for 0% -> 0%
where the time goes in v1:
time: 259 us
  local copies, waits for them, and re-layouts  102 us (39%)
  blocking collectives  79.4 us (31%)
  waiting for transfers between devices  39.8 us (15%)
  between operations  16.1 us (6%)
  matrix products  10.4 us (4%)
  starting transfers between devices  7.43 us (3%)
  other arithmetic  4.05 us (2%)
    while x126, local copies, waits for them, and re-layouts  89.3 us
    all_gather x4, blocking collectives, spread_2(): return jax.lax.all_gather(block, axis_name=axis).sum(axis=0)  79.4 us
    reduce_scatter x1, waiting for transfers between devices, per_device(): lax.psum_scatter(running.reshape(lag_count, c_dev, width_ref), 'seg', sca...  30.4 us
    dot_general x2, matrix products, add_block(): lax.dot_general(lagged, ref_block, (((0,), (0,)), ((), ())), preferred_el...  10.4 us
    all_to_all x1, waiting for transfers between devices, per_device(): lax.all_to_all(my_rows, 'ch', split_axis=1, concat_axis=0, tiled=True)  9.29 us
    all_to_all x1, starting transfers between devices, per_device(): lax.all_to_all(my_rows, 'ch', split_axis=1, concat_axis=0, tiled=True)  7.39 us
  transfers between devices with their start and end apart: 2, of which 2 were waited for; matrix products, arithmetic and copies ran while one was open for 1% of the time, Pallas kernels for 0%

profile of v1, /device:TPU:0, one launch (start us, length us, event | category | flops | bytes accessed | tf_op | source)
XLA Modules:
  0.0 258.8 jit_solution(3589788281017669755)
XLA Ops:
  6.5 1.1 copy.20
  7.7 1.0 copy.13
  8.6 7.4 %all-to-all-start = ((f32[64,16,128]{2,0,1:T(8,128)}), f32[64,16,128]{2,0,1:T(8,128)S(1)}, u32[]{:S(2)}, u32[]{:S(2)}) async-start(f32[64,16,128]{2,0,1:T(8,128)} %copy.13), calls=%async_computation | async-start | bytes 1048576 | tf_op jit(solution)/shard_map/all_to_all | solution.py:39
  16.1 1.5 fusion.3
  20.1 0.8 compare_and_fusion.3
  21.0 9.3 %all-to-all-done = f32[64,16,128]{2,0,1:T(8,128)S(1)} async-done(((f32[64,16,128]{2,0,1:T(8,128)}), f32[64,16,128]{2,0,1:T(8,128)S(1)}, u32[]{:S(2)}, u32[]{:S(2)}) %all-to-all-start) | async-done | bytes 524320 | tf_op jit(solution)/shard_map/all_to_all | solution.py:39
  31.9 21.3 %all-gather.3 = bf16[16384,16]{0,1:T(8,128)(2,1)S(1)} all-gather(bf16[1024,16]{0,1:T(8,128)(2,1)S(1)} %bitcast_select_fusion), channel_id=5, replica_groups=mesh['seg'=2,'ch'=16] {'ch'}, dimensions={0}, use_global_device_ids=true | all-gather | bytes 557056 | tf_op jit(solution)/shard_map/all_gather | solution.py:11
  54.4 18.9 %all-gather.2 = bf16[16384,16]{0,1:T(8,128)(2,1)S(1)} all-gather(bf16[1024,16]{0,1:T(8,128)(2,1)S(1)} %bitcast_select_fusion.1), channel_id=4, replica_groups=mesh['seg'=2,'ch'=16] {'ch'}, dimensions={0}, use_global_device_ids=true | all-gather | bytes 557056 | tf_op jit(solution)/shard_map/all_gather | solution.py:11
  74.4 20.4 %all-gather.1 = bf16[16384,16]{0,1:T(8,128)(2,1)S(1)} all-gather(bf16[1024,16]{0,1:T(8,128)(2,1)S(1)} %bitcast_select_fusion.2), channel_id=3, replica_groups=mesh['seg'=2,'ch'=16] {'ch'}, dimensions={0}, use_global_device_ids=true | all-gather | bytes 557056 | tf_op jit(solution)/shard_map/all_gather | solution.py:11
  96.0 18.9 %all-gather = bf16[16384,16]{0,1:T(8,128)(2,1)S(1)} all-gather(bf16[1024,16]{0,1:T(8,128)(2,1)S(1)} %bitcast_select_fusion.3), channel_id=2, replica_groups=mesh['seg'=2,'ch'=16] {'ch'}, dimensions={0}, use_global_device_ids=true | all-gather | bytes 557056 | tf_op jit(solution)/shard_map/all_gather | solution.py:11
  115.4 101.3 %while.14 = (s32[]{:T(128)}, f32[8192,64]{0,1:T(8,128)S(1)}, bf16[1088,128]{1,0:T(8,128)(2,1)S(1)}, bf16[1024,64]{0,1:T(8,128)(2,1)S(1)}, s32[]{:T(128)}, /*inde...) while((s32[]{:T(128)}, f32[8192,64]{0,1:T(8,128)S(1)}, ...), condition=%wide.region_7.9_spmd.clone, body=%wide.region_6.8_spmd.clone.sunk | while | flops 537919552 | bytes 29427356 | solution.py:61
  120.5 0.8 constant_dynamic-update-slice_fusion.135
  123.3 0.8 constant_dynamic-update-slice_fusion.139
  136.2 0.8 constant_dynamic-update-slice_fusion.157
  160.9 5.2 %convolution_add_fusion.2 = f32[8192,64]{0,1:T(8,128)S(1)} fusion(bf16[512,8192]{1,0:T(8,128)(2,1)} %constant_dynamic-update-slice_fusion.191, f32[8192,64]{0,1:T(8,128)S(1)} %get-tuple-element.243, pred[]{:T(512)S(6)} %compare.4, bf16[1024,64]{0,1:T(8,128)(2,1)S(1)} %get-tuple-element.317, s32[]{:T(128)S(6)} %select_n.98), kind=kOutput, calls=%fused_computation.4.clone.1 | convolution fusion | flops 537919488 | bytes 12648453 | tf_op jit(solution)/shard_map/while/body/eval_jaxpr/dot_general | solution.py:56
  171.1 0.8 constant_dynamic-update-slice_fusion.135
  174.0 0.8 constant_dynamic-update-slice_fusion.139
  186.8 0.8 constant_dynamic-update-slice_fusion.157
  204.4 0.8 constant_dynamic-update-slice_fusion.182
  211.5 5.2 %convolution_add_fusion.2 = f32[8192,64]{0,1:T(8,128)S(1)} fusion(bf16[512,8192]{1,0:T(8,128)(2,1)} %constant_dynamic-update-slice_fusion.191, f32[8192,64]{0,1:T(8,128)S(1)} %get-tuple-element.243, pred[]{:T(512)S(6)} %compare.4, bf16[1024,64]{0,1:T(8,128)(2,1)S(1)} %get-tuple-element.317, s32[]{:T(128)S(6)} %select_n.98), kind=kOutput, calls=%fused_computation.4.clone.1 | convolution fusion | flops 537919488 | bytes 12648453 | tf_op jit(solution)/shard_map/while/body/eval_jaxpr/dot_general | solution.py:56
  216.7 1.7 copy.25
  218.5 30.4 %reduce-scatter.2.cloned.1.call-done = f32[32,128,64]{1,0,2:T(8,128)} async-done(((f32[64,128,64]{1,0,2:T(8,128)}), f32[32,128,64]{1,0,2:T(8,128)}) %reduce-scatter.2.cloned.1.call-update) | async-done | bytes 1048592 | tf_op jit(solution)/shard_map/reduce_scatter | solution.py:62
  248.9 1.4 broadcast_divide_fusion
  250.3 1.6 copy.17
  (155 shorter events, 91.2 us)
Async XLA Ops:
  8.6 21.7 %all-to-all-start = ((f32[64,16,128]{2,0,1:T(8,128)}), f32[64,16,128]{2,0,1:T(8,128)S(1)}, u32[]{:S(2)}, u32[]{:S(2)}) async-start(f32[64,16,128]{2,0,1:T(8,128)} %copy.13), calls=%async_computation | async-start | bytes 1048576 | tf_op jit(solution)/shard_map/all_to_all | solution.py:39
  16.0 232.9 %reduce-scatter.2.cloned.1.call-start = ((), (), s32[]{:S(2)}) async-start(), calls=%async_computation.2 | async-start | bytes 3145728 | tf_op jit(solution)/shard_map/reduce_scatter | solution.py:62
Sparse Core Ops, SparseCore 0:
  218.6 30.2 reduce-scatter.1

commit v2 on v0

--- a/solution.py
+++ b/solution.py
@@ -2,6 +2,7 @@
 import jax.numpy as jnp
 from jax import lax
 from jax.sharding import PartitionSpec as P
+from jax.lax import all_to_all, axis_size
 
 L = 64
 
@@ -36,7 +37,16 @@
     n_seg = lax.axis_size("seg")
     n_total = s_dev * n_ch
     c_dev = chans // n_ch
-    series = lax.all_to_all(my_rows, "ch", split_axis=1, concat_axis=0, tiled=True)
+    treat_the_numbers = lambda axis_name, my_data: jnp.concatenate(
+        all_to_all(
+            jnp.stack(jnp.split(my_data, axis_size(axis_name), 1), 0),
+            axis_name=axis_name,
+            split_axis=0,
+            concat_axis=0,
+        ),
+        0,
+    )
+    series = treat_the_numbers("ch", my_rows)
     detrended = detrend_cols(series)
     panels = owner_panels(detrended, ref_local, owners)
     width_ref = panels.shape[1]

time: 273 us -> 293 us (1.073)
  local copies, waits for them, and re-layouts: 100 us -> 120 us
    unnamed x3 -> x17, local copies, waits for them, and re-layouts: 3 us -> 22.5 us
where the time goes in v2:
time: 293 us; the launch traced here: 292 us
  waiting for transfers between devices  131 us (45%)
  local copies, waits for them, and re-layouts  120 us (41%)
  between operations  16 us (5%)
  matrix products  10.4 us (4%)
  starting transfers between devices  7.47 us (3%)
  other arithmetic  6.21 us (2%)
    while x126, local copies, waits for them, and re-layouts  89.4 us
    psum x1, waiting for transfers between devices, spread_2(): return lax.psum(block, axis)  88.2 us
    reduce_scatter x1, waiting for transfers between devices, per_device(): lax.psum_scatter(running.reshape(lag_count, c_dev, width_ref), 'seg', sca...  33.8 us
    unnamed x17, local copies, waits for them, and re-layouts  22.5 us
    dot_general x2, matrix products, add_block(): lax.dot_general(lagged, ref_block, (((0,), (0,)), ((), ())), preferred_el...  10.4 us
    all_to_all x1, waiting for transfers between devices, per_device(): all_to_all(jnp.stack(jnp.split(my_data, axis_size(axis_name), 1), 0), axi...  9.34 us
    all_to_all x1, starting transfers between devices, per_device(): all_to_all(jnp.stack(jnp.split(my_data, axis_size(axis_name), 1), 0), axi...  7.39 us
  transfers between devices with their start and end apart: 3, of which 3 were waited for; matrix products, arithmetic and copies ran while one was open for 1% of the time, Pallas kernels for 0%

profile of v2, /device:TPU:0, one launch (start us, length us, event | category | flops | bytes accessed | tf_op | source)
XLA Modules:
  0.0 291.9 jit_solution(9256294774244423079)
XLA Ops:
  6.5 1.4 fusion.17
  7.9 1.4 fusion.16
  9.3 1.4 fusion.15
  10.7 1.4 fusion.14
  12.0 1.4 fusion.13
  13.4 1.4 fusion.12
  14.8 1.4 fusion.11
  16.2 1.4 fusion.10
  17.5 1.4 fusion.9
  18.9 1.4 fusion.8
  20.3 1.4 fusion.7
  23.0 1.4 fusion.5
  25.8 1.4 fusion.3
  28.5 7.4 %all-to-all-start = ((f32[16,64,128]{2,1,0:T(8,128)}), f32[16,64,128]{2,1,0:T(8,128)S(1)}, u32[]{:S(2)}, u32[]{:S(2)}) async-start(f32[16,64,128]{2,1,0:T(8,128)} %fusion.2), calls=%async_computation | async-start | bytes 1048576 | tf_op jit(solution)/shard_map/all_to_all | solution.py:41
  36.0 1.5 fusion.19
  40.8 9.3 %all-to-all-done = f32[16,64,128]{2,1,0:T(8,128)S(1)} async-done(((f32[16,64,128]{2,1,0:T(8,128)}), f32[16,64,128]{2,1,0:T(8,128)S(1)}, u32[]{:S(2)}, u32[]{:S(2)}) %all-to-all-start) | async-done | bytes 524320 | tf_op jit(solution)/shard_map/all_to_all | solution.py:41
  56.2 88.2 %all-reduce.4.cloned.1.call-done = (bf16[1024,16]{0,1:T(8,128)(2,1)}, bf16[1024,16]{0,1:T(8,128)(2,1)}, bf16[1024,16]{0,1:T(8,128)(2,1)}, bf16[1024,16]{0,1:T(8,128)(2,1)}) async-done(((bf16[1024,16]{0,1:T(8,128)(2,1)}, bf16[1024,16]{0,1:T(8,128)(2,1)}, bf16[1024,16]{0,1:T(8,128)(2,1)}, bf16[1024,16]{0,1:T(8,128)(2,1)}), (bf16[1024,16]{0,1:T(8,128)(2,1)}, bf16[1024,16]{0,1:T(8,128)(2,1)}, ...) | async-done | bytes 131088 | tf_op jit(solution)/shard_map/psum | solution.py:12
  145.2 101.3 %while.14 = (s32[]{:T(128)}, f32[8192,64]{0,1:T(8,128)S(1)}, bf16[1088,128]{1,0:T(8,128)(2,1)S(1)}, bf16[1024,64]{0,1:T(8,128)(2,1)S(1)}, s32[]{:T(128)}, /*inde...) while((s32[]{:T(128)}, f32[8192,64]{0,1:T(8,128)S(1)}, ...), condition=%wide.region_7.9_spmd.clone, body=%wide.region_6.8_spmd.clone.sunk | while | flops 537919552 | bytes 29427356 | solution.py:71
  190.6 5.2 %convolution_add_fusion.2 = f32[8192,64]{0,1:T(8,128)S(1)} fusion(bf16[512,8192]{1,0:T(8,128)(2,1)} %constant_dynamic-update-slice_fusion.191, f32[8192,64]{0,1:T(8,128)S(1)} %get-tuple-element.245, pred[]{:T(512)S(6)} %compare.4, bf16[1024,64]{0,1:T(8,128)(2,1)S(1)} %get-tuple-element.319, s32[]{:T(128)S(6)} %select_n.98), kind=kOutput, calls=%fused_computation.4.clone.1 | convolution fusion | flops 537919488 | bytes 12648453 | tf_op jit(solution)/shard_map/while/body/eval_jaxpr/dot_general | solution.py:66
  241.3 5.2 %convolution_add_fusion.2 = f32[8192,64]{0,1:T(8,128)S(1)} fusion(bf16[512,8192]{1,0:T(8,128)(2,1)} %constant_dynamic-update-slice_fusion.191, f32[8192,64]{0,1:T(8,128)S(1)} %get-tuple-element.245, pred[]{:T(512)S(6)} %compare.4, bf16[1024,64]{0,1:T(8,128)(2,1)S(1)} %get-tuple-element.319, s32[]{:T(128)S(6)} %select_n.98), kind=kOutput, calls=%fused_computation.4.clone.1 | convolution fusion | flops 537919488 | bytes 12648453 | tf_op jit(solution)/shard_map/while/body/eval_jaxpr/dot_general | solution.py:66
  246.5 1.7 copy.13
  248.2 33.8 %reduce-scatter.2.cloned.1.call-done = f32[32,128,64]{1,0,2:T(8,128)} async-done(((f32[64,128,64]{1,0,2:T(8,128)}), f32[32,128,64]{1,0,2:T(8,128)}) %reduce-scatter.2.cloned.1.call-update) | async-done | bytes 1048592 | tf_op jit(solution)/shard_map/reduce_scatter | solution.py:72
  282.1 1.4 broadcast_divide_fusion
  283.5 1.6 copy.10
  (157 shorter events, 102.6 us)
Async XLA Ops:
  28.5 21.7 %all-to-all-start = ((f32[16,64,128]{2,1,0:T(8,128)}), f32[16,64,128]{2,1,0:T(8,128)S(1)}, u32[]{:S(2)}, u32[]{:S(2)}) async-start(f32[16,64,128]{2,1,0:T(8,128)} %fusion.2), calls=%async_computation | async-start | bytes 1048576 | tf_op jit(solution)/shard_map/all_to_all | solution.py:41
  35.9 108.4 %all-reduce.4.cloned.1.call-start = ((), (), s32[]{:S(2)}) async-start(), calls=%async_computation.3 | async-start | bytes 262144 | tf_op jit(solution)/shard_map/psum | solution.py:12
  55.9 226.2 %reduce-scatter.2.cloned.1.call-start = ((), (), s32[]{:S(2)}) async-start(), calls=%async_computation.2 | async-start | bytes 3145728 | tf_op jit(solution)/shard_map/reduce_scatter | solution.py:72
Sparse Core Ops, SparseCore 0:
  56.0 88.2 all-reduce.3
  248.3 33.6 reduce-scatter.1
